TPU v7x, 32 devices: a whole 2x2x4 slice. The times are simulated.
32 devices in a mesh: section: 8 (over y, x, core), rep: 4 (over z).
Axes of the slice: x: 2, y: 2, z: 4, core: 2. Of those that a mesh axis runs over, the one named last changes fastest.
Arguments:
- features: bfloat16 [16384, 128], P('section'), may hold values from -6 to 6
- order: int32 [16384], P('section'), may hold values from 0 to 2047, as said below
- tiles: bfloat16 [8, 4, 2, 96, 128, 128], P('section', 'rep'), may hold values from -0.125 to 0.125
- tile_rows: int32 [8, 4, 2, 96], P('section', 'rep'), may hold values from 0 to 15, as said below
- tile_cols: int32 [8, 4, 2, 96], P('section', 'rep'), may hold values from 0 to 15, as said below
- live: int32 [8, 4, 2], P('section', 'rep'), may hold values from 1 to 96, as said below
- weight: bfloat16 [128, 128], replicated, may hold values from -0.5 to 0.5
- cotangent: bfloat16 [16384, 128], P('section'), may hold values from -6 to 6
Outputs:
- hidden: bfloat16 [16384, 128], P('section')
- weight_grad: float32 [128, 128], replicated
- feature_grad: bfloat16 [16384, 128], P('section')
Inputs may be any that keep to these rules, and one draw needn't show every extreme that they name: `order`: within each panel of 2048 rows, a permutation of the local row numbers. For one section, replica and round, the 96 pairs (tile_rows, tile_cols) are distinct. `tile_cols`: block column within the panel j * 4 + r for replica r and round j. Some section, replica and round has all 96 slots live.
All inputs are finite; a program needn't handle non-finite values.
Results may differ from a plain program's by a relative error of at most 0.012.
Values may be sent and summed in bfloat16 or wider, within the bound.
No kernel may reach another device: no remote copies, remote signals or barrier semaphores. Data moves between devices by JAX's collectives and lax.ppermute only.
A program may use at most 192 MiB of HBM per device.

v0:
```python
import math
import jax
import jax.numpy as jnp
from jax import lax
from jax.sharding import PartitionSpec as P


def spread(value, axis, source):
    kept = jnp.where(lax.axis_index(axis) == source, value, 0).astype(value.dtype)
    return lax.psum(kept, axis)


def shards(features, order, tiles, tile_rows, tile_cols, live, weight, cotangent):
    rep_count = lax.axis_size("rep")
    section_count = lax.axis_size("section")
    rep_index = lax.axis_index("rep")
    section_index = lax.axis_index("section")
    panel_rows, width = features.shape
    block_rows = tiles.shape[-1]
    blocks = panel_rows // block_rows
    rounds = tiles.shape[2]
    slot_count = tiles.shape[3]
    own_tiles = tiles[0, 0]
    row_table = tile_rows[0, 0]
    col_table = tile_cols[0, 0]
    live_counts = live[0, 0]
    slot_ids = jnp.arange(slot_count, dtype=jnp.int32)
    block_ids = jnp.arange(blocks, dtype=jnp.int32)
    grad_scale = 1.0 / math.sqrt(panel_rows * section_count)
    reordered = jnp.take(features, order, axis=0)

    def forward_round(round_no, running):
        root = round_no * rep_count + rep_index
        panel = spread(reordered, "section", root)
        tile_set = lax.dynamic_index_in_dim(own_tiles, round_no, 0, keepdims=False)
        row_ids = lax.dynamic_index_in_dim(row_table, round_no, 0, keepdims=False)
        col_ids = lax.dynamic_index_in_dim(col_table, round_no, 0, keepdims=False)
        count_now = lax.dynamic_index_in_dim(live_counts, round_no, 0, keepdims=False)
        picked = jnp.take(panel.reshape(blocks, block_rows, width), col_ids, axis=0)
        products = jnp.einsum("kab,kbf->kaf", tile_set, picked, preferred_element_type=jnp.float32)
        select = (
            (row_ids[None, :] == block_ids[:, None]) & (slot_ids < count_now)[None, :]
        ).astype(jnp.float32)
        return running + jnp.einsum(
            "pk,kaf->paf", select, products, precision=lax.Precision.HIGHEST
        )

    partial_sum = lax.fori_loop(
        0, rounds, forward_round, jnp.zeros((blocks, block_rows, width), jnp.float32)
    )
    partial_sum = partial_sum.reshape(panel_rows, width)
    share_rows = panel_rows // rep_count
    row_share = lax.psum_scatter(partial_sum, "rep", scatter_dimension=0, tiled=True)
    co_share = lax.dynamic_slice_in_dim(cotangent, rep_index * share_rows, share_rows, 0)
    aggregated = row_share.astype(jnp.bfloat16)
    preact = jnp.dot(aggregated, weight, preferred_element_type=jnp.float32)
    out_rows = jax.nn.silu(preact).astype(jnp.bfloat16)
    sigmoid_part = jax.nn.sigmoid(preact)
    grad_pre = (
        co_share.astype(jnp.float32) * sigmoid_part * (1.0 + preact * (1.0 - sigmoid_part))
    ).astype(jnp.bfloat16)
    grad_part = jnp.einsum("nf,ng->fg", aggregated, grad_pre, preferred_element_type=jnp.float32)
    up_rows = jnp.einsum("ng,fg->nf", grad_pre, weight, preferred_element_type=jnp.float32).astype(
        jnp.bfloat16
    )
    hidden_share, grad_part, upstream_share = (out_rows, grad_part, up_rows)
    weight_grad = lax.psum(grad_part, ("section", "rep")) * grad_scale
    hidden, upstream = (
        lax.all_gather(hidden_share, "rep", axis=0, tiled=True),
        lax.all_gather(upstream_share, "rep", axis=0, tiled=True),
    )
    up_blocks = upstream.reshape(blocks, block_rows, width)
    picked_up = jnp.take(up_blocks, row_table.reshape(-1), axis=0).reshape(
        rounds, slot_count, block_rows, width
    )
    products_back = jnp.einsum(
        "jkab,jkaf->jkbf", own_tiles, picked_up, preferred_element_type=jnp.float32
    )
    alive_mask = slot_ids[None, None, :] < live_counts[:, None, None]
    select_back = ((col_table[:, None, :] == block_ids[None, :, None]) & alive_mask).astype(
        jnp.float32
    )
    contrib = jnp.einsum(
        "jpk,jkbf->jpbf", select_back, products_back, precision=lax.Precision.HIGHEST
    )
    contrib = lax.optimization_barrier(contrib.astype(jnp.bfloat16)).astype(jnp.float32)
    contrib = contrib.reshape(rounds, panel_rows, width)
    totals = lax.psum(contrib.astype(jnp.bfloat16), "section").astype(jnp.float32)
    own_panel = lax.dynamic_index_in_dim(
        totals, section_index // rep_count, 0, keepdims=False
    ).astype(jnp.bfloat16)
    grad_rows = spread(own_panel, "rep", section_index % rep_count)
    feature_grad = jnp.zeros_like(features).at[order].set(grad_rows)
    return (hidden, weight_grad, feature_grad)


def solution(mesh):
    placed = (
        P("section", None),
        P("section"),
        P("section", "rep", None, None, None, None),
        P("section", "rep", None, None),
        P("section", "rep", None, None),
        P("section", "rep", None),
        P(),
        P("section", None),
    )
    return jax.shard_map(
        shards,
        mesh=mesh,
        in_specs=placed,
        out_specs=(P("section", None), P(), P("section", None)),
        check_vma=False,
    )
```

profile of v0, /device:TPU:0, one launch (start us, length us, event | category | flops | bytes accessed | tf_op | source)
XLA Modules:
  0.0 487.0 jit_solution(13288153377587932532)
XLA Ops:
  9.5 6.2 %gather_fusion.1 = bf16[2048,128]{1,0:T(8,128)(2,1)S(1)} fusion(bf16[2048,128]{1,0:T(8,128)(2,1)S(1)} %copy-done, s32[2048]{0:T(1024)S(1)} %get-tuple-element.296), kind=kCustom, calls=%fused_computation.1 | custom fusion | bytes 1056768 | tf_op jit(solution)/shard_map/jit(_take)/gather | solution.py:30
  16.0 147.6 %while.16 = (s32[]{:T(128)}, f32[16,128,128]{2,0,1:T(8,128)S(1)}, s32[2,96]{1,0:T(2,128)}, s32[2]{0:T(128)}, bf16[2,96,128,128]{3,2,1,0:T(8,128)(2,1)}, /*index=...) while((s32[]{:T(128)}, f32[16,128,128]{2,0,1:T(8,128)S(1)}, ...), condition=%wide.region_2.3_spmd.clone, body=%wide.region_0.0_spmd.clone.sunk | while | flops 707269568 | bytes 31465112 | solution.py:48
  16.1 0.8 broadcast_select_fusion.3
  18.3 1.2 dynamic_slice.80
  20.9 57.2 %all-reduce.11.cloned.1.call-done = bf16[16,128,128]{2,1,0:T(8,128)(2,1)} async-done(((bf16[16,128,128]{2,1,0:T(8,128)(2,1)}), bf16[16,128,128]{2,1,0:T(8,128)(2,1)}) %all-reduce.11.cloned.1.call-update) | async-done | bytes 524304 | tf_op jit(solution)/shard_map/while/body/eval_jaxpr/psum | solution.py:10
  78.1 3.7 gather_fusion
  81.9 3.9 fusion.65
  85.8 5.7 %fusion.67 = f32[16,128,128]{2,0,1:T(8,128)S(1)} fusion(f32[96,128,128]{2,1,0:T(8,128)S(1)} %fusion.65, f32[16,128,128]{2,0,1:T(8,128)S(1)} %get-tuple-element.360, pred[]{:T(512)S(6)} %compare.6, s32[96]{0:T(128)S(1)} %fusion.66, pred[96]{0:T(512)(128)(4,1)S(1)} %iota_compare_fusion.5), kind=kOutput, calls=%fused_computation.14.clone.1 | convolution fusion | flops 302517248 | bytes 8389089 | tf_op jit(solution)/shard_map/while/body/eval_jaxpr/pk,kaf->paf/dot_general | solution.py:44
  91.6 0.8 broadcast_select_fusion.3
  93.8 1.2 dynamic_slice.80
  96.4 53.8 %all-reduce.11.cloned.1.call-done = bf16[16,128,128]{2,1,0:T(8,128)(2,1)} async-done(((bf16[16,128,128]{2,1,0:T(8,128)(2,1)}), bf16[16,128,128]{2,1,0:T(8,128)(2,1)}) %all-reduce.11.cloned.1.call-update) | async-done | bytes 524304 | tf_op jit(solution)/shard_map/while/body/eval_jaxpr/psum | solution.py:10
  150.2 3.7 gather_fusion
  154.0 3.9 fusion.65
  157.9 5.7 %fusion.67 = f32[16,128,128]{2,0,1:T(8,128)S(1)} fusion(f32[96,128,128]{2,1,0:T(8,128)S(1)} %fusion.65, f32[16,128,128]{2,0,1:T(8,128)S(1)} %get-tuple-element.360, pred[]{:T(512)S(6)} %compare.6, s32[96]{0:T(128)S(1)} %fusion.66, pred[96]{0:T(512)(128)(4,1)S(1)} %iota_compare_fusion.5), kind=kOutput, calls=%fused_computation.14.clone.1 | convolution fusion | flops 302517248 | bytes 8389089 | tf_op jit(solution)/shard_map/while/body/eval_jaxpr/pk,kaf->paf/dot_general | solution.py:44
  163.7 1.3 copy.11
  167.3 25.6 %reduce-scatter.2.cloned.1.call-done = f32[512,128]{1,0:T(8,128)} async-done(((f32[2048,128]{1,0:T(8,128)}), f32[512,128]{1,0:T(8,128)}) %reduce-scatter.2.cloned.1.call-update) | async-done | bytes 262160 | tf_op jit(solution)/shard_map/reduce_scatter | solution.py:53
  192.9 1.3 multiply_convert_fusion
  194.3 16.2 %all_gather.7 = bf16[2048,128]{1,0:T(8,128)(2,1)S(1)} all-gather(bf16[512,128]{1,0:T(8,128)(2,1)S(1)} %convolution_convert_fusion), channel_id=1, replica_groups=mesh['section'=8,'rep'=4] {'rep'}, dimensions={0}, use_global_device_ids=true | all-gather | bytes 655360 | tf_op jit(solution)/shard_map/all_gather | solution.py:70
  210.5 8.0 %gather_fusion.2 = bf16[192,128,128]{2,1,0:T(8,128)(2,1)} fusion(bf16[16,128,128]{2,1,0:T(8,128)(2,1)S(1)} %bitcast.60, s32[1024]{0:T(1024)S(1)} %pad_clamp_fusion.1), kind=kCustom, calls=%fused_computation.2 | custom fusion | bytes 12583680 | tf_op jit(solution)/shard_map/jit(_take)/gather | solution.py:73
  218.5 11.6 %fusion.26 = f32[2,96,128,128]{3,2,1,0:T(8,128)} fusion(bf16[2,96,128,128]{3,2,1,0:T(8,128)(2,1)} %bitcast.64, pred[2,96]{1,0:T(4,128)(4,1)S(1)} %compare_and_fusion.2, bf16[1,1,2,96,128,128]{5,4,3,2,1,0:T(8,128)(2,1)} %bitcast.62), kind=kOutput, calls=%fused_computation.34 | convolution fusion | flops 808452096 | bytes 25166016 | tf_op jit(solution)/shard_map/jkab,jkaf->jkbf/dot_general | solution.py:76
  230.1 12.8 %copy.14 = f32[2,96,128,128]{2,1,3,0:T(8,128)} copy(f32[2,96,128,128]{3,2,1,0:T(8,128)} %fusion.26) | data formatting | bytes 25165824 | tf_op jit(solution)/shard_map/jkab,jkaf->jkbf/dot_general | solution.py:76
  242.8 7.2 %fusion.30 = bf16[2,16,128,128]{3,1,2,0:T(8,128)(2,1)S(1)} fusion(f32[2,96,128,128]{2,1,3,0:T(8,128)} %copy.14, s32[2,96]{1,0:T(2,128)S(1)} %copy-done.3, pred[2,96]{1,0:T(4,128)(4,1)S(1)} %iota_compare_fusion.3), kind=kOutput, calls=%fused_computation.38 | convolution fusion | flops 604510208 | bytes 13632448 | tf_op jit(solution)/shard_map/jpk,jkbf->jpbf/dot_general | solution.py:83
  250.1 1.3 copy.12
  251.5 0.9 fusion.37
  252.5 53.3 %all-reduce.7.cloned.1.call-done = bf16[2,2048,128]{2,1,0:T(8,128)(2,1)} async-done(((bf16[2,2048,128]{2,1,0:T(8,128)(2,1)}), bf16[2,2048,128]{2,1,0:T(8,128)(2,1)}) %all-reduce.7.cloned.1.call-update) | async-done | bytes 1048592 | tf_op jit(solution)/shard_map/psum | solution.py:88
  305.8 1.9 fusion.34
  307.7 14.8 %all_gather.6 = bf16[2048,128]{1,0:T(8,128)(2,1)S(1)} all-gather(bf16[512,128]{1,0:T(8,128)(2,1)S(1)} %get-tuple-element.294), channel_id=1, replica_groups=mesh['section'=8,'rep'=4] {'rep'}, dimensions={0}, use_global_device_ids=true | all-gather | bytes 655360 | tf_op jit(solution)/shard_map/all_gather | solution.py:69
  322.5 106.7 %all-reduce.5.cloned.1.call-done = f32[128,128]{1,0:T(8,128)} async-done(((f32[128,128]{1,0:T(8,128)}), f32[128,128]{1,0:T(8,128)}) %all-reduce.5.cloned.1.call-update) | async-done | bytes 65552 | tf_op jit(solution)/shard_map/psum | solution.py:67
  429.3 1.5 broadcast_multiply_fusion
  430.7 41.1 %all-reduce.9.cloned.1.call-done = bf16[2048,128]{1,0:T(8,128)(2,1)} async-done(((bf16[2048,128]{1,0:T(8,128)(2,1)}), bf16[2048,128]{1,0:T(8,128)(2,1)}) %all-reduce.9.cloned.1.call-update) | async-done | bytes 524304 | tf_op jit(solution)/shard_map/psum | solution.py:10
  471.8 6.8 %scatter_custom_fusion = bf16[2048,128]{1,0:T(8,128)(2,1)} fusion(s32[2048]{0:T(1024)S(1)} %get-tuple-element.295, bf16[2048,128]{1,0:T(8,128)(2,1)} %all-reduce.9.cloned.1.call-done, bf16[]{:T(256)} %constant.190.clone.1), kind=kCustom, calls=%fused_computation.44 | custom fusion | bytes 524800 | tf_op jit(solution)/shard_map/scatter | solution.py:93
  478.7 0.8 copy.33
  (40 shorter events, 10.0 us)
Async XLA Ops:
  8.0 1.5 copy-start
  16.0 176.9 %copy-start.2 = (bf16[128,128]{1,0:T(8,128)(2,1)S(1)}, bf16[128,128]{1,0:T(8,128)(2,1)}, u32[]{:S(2)}) copy-start(bf16[128,128]{1,0:T(8,128)(2,1)} %param.16) | copy-start | bytes 98308
  16.0 62.1 %all-reduce.11.cloned.1.call-start = ((), (), s32[]{:S(2)}) async-start(), calls=%async_computation.5 | async-start | bytes 1048576 | tf_op jit(solution)/shard_map/while/body/eval_jaxpr/psum | solution.py:10
  91.5 58.7 %all-reduce.11.cloned.1.call-start = ((), (), s32[]{:S(2)}) async-start(), calls=%async_computation.5 | async-start | bytes 1048576 | tf_op jit(solution)/shard_map/while/body/eval_jaxpr/psum | solution.py:10
  163.6 29.2 %reduce-scatter.2.cloned.1.call-start = ((), (), s32[]{:S(2)}) async-start(), calls=%async_computation.1 | async-start | bytes 1310720 | tf_op jit(solution)/shard_map/reduce_scatter | solution.py:53
  165.0 140.7 %all-reduce.7.cloned.1.call-start = ((), (), s32[]{:S(2)}) async-start(), calls=%async_computation.3 | async-start | bytes 2097152 | tf_op jit(solution)/shard_map/psum | solution.py:88
  230.1 12.8 %copy-start.3 = (s32[2,96]{1,0:T(2,128)S(1)}, s32[2,96]{1,0:T(2,128)}, u32[]{:S(2)}) copy-start(s32[2,96]{1,0:T(2,128)} %get-tuple-element.411) | copy-start | bytes 2308
  242.8 8.7 %copy-start.1 = (f32[512,128]{1,0:T(8,128)S(1)}, f32[512,128]{1,0:T(8,128)}, u32[]{:S(2)}) copy-start(f32[512,128]{1,0:T(8,128)} %reduce-scatter.2.cloned.1.call-done) | copy-start | bytes 786436
  251.4 177.8 %all-reduce.5.cloned.1.call-start = ((), (), s32[]{:S(2)}) async-start(), calls=%async_computation.2 | async-start | bytes 131072 | tf_op jit(solution)/shard_map/psum | solution.py:67
  252.4 219.4 %all-reduce.9.cloned.1.call-start = ((), (), s32[]{:S(2)}) async-start(), calls=%async_computation.4 | async-start | bytes 1048576 | tf_op jit(solution)/shard_map/psum | solution.py:10
Sparse Core Ops, SparseCore 0:
  20.8 57.2 all-reduce.10
  96.3 53.8 all-reduce.10
Sparse Core Ops, SparseCore 1:
  166.4 26.4 reduce-scatter.1
  251.5 54.2 all-reduce.6
  312.7 116.5 all-reduce.4
  432.3 39.4 all-reduce.8
where the time goes:
time: 488 us; the launch traced here: 487 us
  waiting for transfers between devices  338 us (69%)
  local copies, waits for them, and re-layouts  49.3 us (10%)
  matrix products  40.4 us (8%)
  blocking collectives  31 us (6%)
  between operations  15.8 us (3%)
  other arithmetic  12.4 us (3%)
    psum x3, waiting for transfers between devices, spread(): return lax.psum(kept, axis)  152 us
    psum x1, waiting for transfers between devices, shards(): weight_grad = lax.psum(grad_part, ('section', 'rep')) * grad_scale  107 us
    psum x1, waiting for transfers between devices, shards(): lax.psum(contrib.astype(jnp.bfloat16), 'section').astype(jnp.float32)  53.3 us
    reduce_scatter x1, waiting for transfers between devices, shards(): lax.psum_scatter(partial_sum, 'rep', scatter_dimension=0, tiled=True)  25.6 us
    all_gather x1, blocking collectives, shards(): lax.all_gather(upstream_share, 'rep', axis=0, tiled=True)  16.2 us
    all_gather x1, blocking collectives, shards(): lax.all_gather(hidden_share, 'rep', axis=0, tiled=True)  14.8 us
    dot_general x1, local copies, waits for them, and re-layouts, shards(): jnp.einsum('jkab,jkaf->jkbf', own_tiles, picked_up, preferred_element_typ...  12.8 us
    dot_general x1, matrix products, shards(): jnp.einsum('jkab,jkaf->jkbf', own_tiles, picked_up, preferred_element_typ...  11.6 us
  transfers between devices with their start and end apart: 6, of which 6 were waited for; matrix products, arithmetic and copies ran while one was open for 3% of the time, Pallas kernels for 0%

commit v1 on v0

--- a/solution.py
+++ b/solution.py
@@ -3,6 +3,12 @@
 import jax.numpy as jnp
 from jax import lax
 from jax.sharding import PartitionSpec as P
+
+
+def seats_all_unite(vals):
+    a_now = jax.lax.psum(vals, axis_name="rep")
+    after = jax.lax.psum(a_now, axis_name="section")
+    return after
 
 
 def spread(value, axis, source):
@@ -64,7 +70,7 @@
         jnp.bfloat16
     )
     hidden_share, grad_part, upstream_share = (out_rows, grad_part, up_rows)
-    weight_grad = lax.psum(grad_part, ("section", "rep")) * grad_scale
+    weight_grad = seats_all_unite(grad_part) * grad_scale
     hidden, upstream = (
         lax.all_gather(hidden_share, "rep", axis=0, tiled=True),
         lax.all_gather(upstream_share, "rep", axis=0, tiled=True),

time: 488 us -> 446 us (0.914)
  waiting for transfers between devices: 338 us -> 296 us
    psum x1 -> x2, waiting for transfers between devices: 107 us -> 61.2 us  [the longest x1 37.8 us: seats_all_unite(): after = jax.lax.psum(a_now, axis_name='section')]
    psum x1, waiting for transfers between devices: 53.3 us -> 58.6 us  [shards(): lax.psum(contrib.astype(jnp.bfloat16), 'section').astype(jnp.float32)]
  transfers between devices with their start and end apart: 6 -> 7, of which waited for: 6 -> 7; matrix products, arithmetic and copies ran while one was open for 3% -> 5% of each run, Pallas kernels for 0% -> 0%
where the time goes in v1:
time: 446 us; the launch traced here: 445 us
  waiting for transfers between devices  296 us (66%)
  local copies, waits for them, and re-layouts  49.3 us (11%)
  matrix products  40.3 us (9%)
  blocking collectives  30.9 us (7%)
  between operations  15.8 us (4%)
  other arithmetic  12.4 us (3%)
    psum x3, waiting for transfers between devices, spread(): return lax.psum(kept, axis)  151 us
    psum x1, waiting for transfers between devices, shards(): lax.psum(contrib.astype(jnp.bfloat16), 'section').astype(jnp.float32)  58.6 us
    psum x1, waiting for transfers between devices, seats_all_unite(): after = jax.lax.psum(a_now, axis_name='section')  37.8 us
    reduce_scatter x1, waiting for transfers between devices, shards(): lax.psum_scatter(partial_sum, 'rep', scatter_dimension=0, tiled=True)  25.6 us
    psum x1, waiting for transfers between devices, seats_all_unite(): a_now = jax.lax.psum(vals, axis_name='rep')  23.4 us
    all_gather x1, blocking collectives, shards(): lax.all_gather(upstream_share, 'rep', axis=0, tiled=True)  16.2 us
    all_gather x1, blocking collectives, shards(): lax.all_gather(hidden_share, 'rep', axis=0, tiled=True)  14.7 us
    dot_general x1, local copies, waits for them, and re-layouts, shards(): jnp.einsum('jkab,jkaf->jkbf', own_tiles, picked_up, preferred_element_typ...  12.8 us
  transfers between devices with their start and end apart: 7, of which 7 were waited for; matrix products, arithmetic and copies ran while one was open for 5% of the time, Pallas kernels for 0%

profile of v1, /device:TPU:0, one launch (start us, length us, event | category | flops | bytes accessed | tf_op | source)
XLA Modules:
  0.0 445.5 jit_solution(15518854962776417311)
XLA Ops:
  9.5 6.2 %gather_fusion.1 = bf16[2048,128]{1,0:T(8,128)(2,1)S(1)} fusion(bf16[2048,128]{1,0:T(8,128)(2,1)S(1)} %copy-done, s32[2048]{0:T(1024)S(1)} %get-tuple-element.296), kind=kCustom, calls=%fused_computation.1 | custom fusion | bytes 1056768 | tf_op jit(solution)/shard_map/jit(_take)/gather | solution.py:36
  16.0 147.6 %while.16 = (s32[]{:T(128)}, f32[16,128,128]{2,0,1:T(8,128)S(1)}, s32[2,96]{1,0:T(2,128)}, s32[2]{0:T(128)}, bf16[2,96,128,128]{3,2,1,0:T(8,128)(2,1)}, /*index=...) while((s32[]{:T(128)}, f32[16,128,128]{2,0,1:T(8,128)S(1)}, ...), condition=%wide.region_2.3_spmd.clone, body=%wide.region_0.0_spmd.clone.sunk | while | flops 707269568 | bytes 31465112 | solution.py:54
  16.1 0.8 broadcast_select_fusion.3
  18.3 1.2 dynamic_slice.80
  20.9 57.2 %all-reduce.14.cloned.1.call-done = bf16[16,128,128]{2,1,0:T(8,128)(2,1)} async-done(((bf16[16,128,128]{2,1,0:T(8,128)(2,1)}), bf16[16,128,128]{2,1,0:T(8,128)(2,1)}) %all-reduce.14.cloned.1.call-update) | async-done | bytes 524304 | tf_op jit(solution)/shard_map/while/body/eval_jaxpr/psum | solution.py:16
  78.1 3.7 gather_fusion
  81.9 3.9 fusion.65
  85.8 5.7 %fusion.67 = f32[16,128,128]{2,0,1:T(8,128)S(1)} fusion(f32[96,128,128]{2,1,0:T(8,128)S(1)} %fusion.65, f32[16,128,128]{2,0,1:T(8,128)S(1)} %get-tuple-element.360, pred[]{:T(512)S(6)} %compare.6, s32[96]{0:T(128)S(1)} %fusion.66, pred[96]{0:T(512)(128)(4,1)S(1)} %iota_compare_fusion.5), kind=kOutput, calls=%fused_computation.14.clone.1 | convolution fusion | flops 302517248 | bytes 8389089 | tf_op jit(solution)/shard_map/while/body/eval_jaxpr/pk,kaf->paf/dot_general | solution.py:50
  91.6 0.8 broadcast_select_fusion.3
  93.8 1.2 dynamic_slice.80
  96.4 53.8 %all-reduce.14.cloned.1.call-done = bf16[16,128,128]{2,1,0:T(8,128)(2,1)} async-done(((bf16[16,128,128]{2,1,0:T(8,128)(2,1)}), bf16[16,128,128]{2,1,0:T(8,128)(2,1)}) %all-reduce.14.cloned.1.call-update) | async-done | bytes 524304 | tf_op jit(solution)/shard_map/while/body/eval_jaxpr/psum | solution.py:16
  150.2 3.7 gather_fusion
  154.0 3.9 fusion.65
  157.9 5.7 %fusion.67 = f32[16,128,128]{2,0,1:T(8,128)S(1)} fusion(f32[96,128,128]{2,1,0:T(8,128)S(1)} %fusion.65, f32[16,128,128]{2,0,1:T(8,128)S(1)} %get-tuple-element.360, pred[]{:T(512)S(6)} %compare.6, s32[96]{0:T(128)S(1)} %fusion.66, pred[96]{0:T(512)(128)(4,1)S(1)} %iota_compare_fusion.5), kind=kOutput, calls=%fused_computation.14.clone.1 | convolution fusion | flops 302517248 | bytes 8389089 | tf_op jit(solution)/shard_map/while/body/eval_jaxpr/pk,kaf->paf/dot_general | solution.py:50
  163.7 1.3 copy.11
  167.3 25.6 %reduce-scatter.2.cloned.1.call-done = f32[512,128]{1,0:T(8,128)} async-done(((f32[2048,128]{1,0:T(8,128)}), f32[512,128]{1,0:T(8,128)}) %reduce-scatter.2.cloned.1.call-update) | async-done | bytes 262160 | tf_op jit(solution)/shard_map/reduce_scatter | solution.py:59
  192.9 1.3 multiply_convert_fusion
  194.3 16.2 %all_gather.7 = bf16[2048,128]{1,0:T(8,128)(2,1)S(1)} all-gather(bf16[512,128]{1,0:T(8,128)(2,1)S(1)} %convolution_convert_fusion), channel_id=1, replica_groups=mesh['section'=8,'rep'=4] {'rep'}, dimensions={0}, use_global_device_ids=true | all-gather | bytes 655360 | tf_op jit(solution)/shard_map/all_gather | solution.py:76
  210.5 8.0 %gather_fusion.2 = bf16[192,128,128]{2,1,0:T(8,128)(2,1)} fusion(bf16[16,128,128]{2,1,0:T(8,128)(2,1)S(1)} %bitcast.60, s32[1024]{0:T(1024)S(1)} %pad_clamp_fusion.1), kind=kCustom, calls=%fused_computation.2 | custom fusion | bytes 12583680 | tf_op jit(solution)/shard_map/jit(_take)/gather | solution.py:79
  218.6 11.5 %fusion.26 = f32[2,96,128,128]{3,2,1,0:T(8,128)} fusion(bf16[2,96,128,128]{3,2,1,0:T(8,128)(2,1)} %bitcast.64, pred[2,96]{1,0:T(4,128)(4,1)S(1)} %compare_and_fusion.2, bf16[1,1,2,96,128,128]{5,4,3,2,1,0:T(8,128)(2,1)} %bitcast.62), kind=kOutput, calls=%fused_computation.34 | convolution fusion | flops 808452096 | bytes 25166016 | tf_op jit(solution)/shard_map/jkab,jkaf->jkbf/dot_general | solution.py:82
  230.1 12.8 %copy.14 = f32[2,96,128,128]{2,1,3,0:T(8,128)} copy(f32[2,96,128,128]{3,2,1,0:T(8,128)} %fusion.26) | data formatting | bytes 25165824 | tf_op jit(solution)/shard_map/jkab,jkaf->jkbf/dot_general | solution.py:82
  242.9 0.9 fusion.37
  243.8 7.2 %fusion.30 = bf16[2,16,128,128]{3,1,2,0:T(8,128)(2,1)S(1)} fusion(f32[2,96,128,128]{2,1,3,0:T(8,128)} %copy.14, s32[2,96]{1,0:T(2,128)S(1)} %copy-done.3, pred[2,96]{1,0:T(4,128)(4,1)S(1)} %iota_compare_fusion.3), kind=kOutput, calls=%fused_computation.38 | convolution fusion | flops 604510208 | bytes 13632448 | tf_op jit(solution)/shard_map/jpk,jkbf->jpbf/dot_general | solution.py:89
  251.0 1.3 copy.12
  252.4 23.4 %all-reduce.6.cloned.1.call-done = f32[128,128]{1,0:T(8,128)} async-done(((f32[128,128]{1,0:T(8,128)}), f32[128,128]{1,0:T(8,128)}) %all-reduce.6.cloned.1.call-update) | async-done | bytes 65552 | tf_op jit(solution)/shard_map/psum | solution.py:9
  275.9 58.6 %all-reduce.10.cloned.1.call-done = bf16[2,2048,128]{2,1,0:T(8,128)(2,1)} async-done(((bf16[2,2048,128]{2,1,0:T(8,128)(2,1)}), bf16[2,2048,128]{2,1,0:T(8,128)(2,1)}) %all-reduce.10.cloned.1.call-update) | async-done | bytes 1048592 | tf_op jit(solution)/shard_map/psum | solution.py:94
  334.5 1.9 fusion.34
  336.5 14.7 %all_gather.6 = bf16[2048,128]{1,0:T(8,128)(2,1)S(1)} all-gather(bf16[512,128]{1,0:T(8,128)(2,1)S(1)} %get-tuple-element.294), channel_id=1, replica_groups=mesh['section'=8,'rep'=4] {'rep'}, dimensions={0}, use_global_device_ids=true | all-gather | bytes 655360 | tf_op jit(solution)/shard_map/all_gather | solution.py:75
  351.2 37.8 %all-reduce.8.cloned.1.call-done = f32[128,128]{1,0:T(8,128)} async-done(((f32[128,128]{1,0:T(8,128)}), f32[128,128]{1,0:T(8,128)}) %all-reduce.8.cloned.1.call-update) | async-done | bytes 65552 | tf_op jit(solution)/shard_map/psum | solution.py:10
  389.0 1.5 broadcast_multiply_fusion
  390.5 39.7 %all-reduce.12.cloned.1.call-done = bf16[2048,128]{1,0:T(8,128)(2,1)} async-done(((bf16[2048,128]{1,0:T(8,128)(2,1)}), bf16[2048,128]{1,0:T(8,128)(2,1)}) %all-reduce.12.cloned.1.call-update) | async-done | bytes 524304 | tf_op jit(solution)/shard_map/psum | solution.py:16
  430.3 6.8 %scatter_custom_fusion = bf16[2048,128]{1,0:T(8,128)(2,1)} fusion(s32[2048]{0:T(1024)S(1)} %get-tuple-element.295, bf16[2048,128]{1,0:T(8,128)(2,1)} %all-reduce.12.cloned.1.call-done, bf16[]{:T(256)} %constant.190.clone.1), kind=kCustom, calls=%fused_computation.44 | custom fusion | bytes 524800 | tf_op jit(solution)/shard_map/scatter | solution.py:99
  (43 shorter events, 10.9 us)
Async XLA Ops:
  8.0 1.5 copy-start
  16.0 176.9 %copy-start.2 = (bf16[128,128]{1,0:T(8,128)(2,1)S(1)}, bf16[128,128]{1,0:T(8,128)(2,1)}, u32[]{:S(2)}) copy-start(bf16[128,128]{1,0:T(8,128)(2,1)} %param.16) | copy-start | bytes 98308
  16.0 62.1 %all-reduce.14.cloned.1.call-start = ((), (), s32[]{:S(2)}) async-start(), calls=%async_computation.6 | async-start | bytes 1048576 | tf_op jit(solution)/shard_map/while/body/eval_jaxpr/psum | solution.py:16
  91.5 58.7 %all-reduce.14.cloned.1.call-start = ((), (), s32[]{:S(2)}) async-start(), calls=%async_computation.6 | async-start | bytes 1048576 | tf_op jit(solution)/shard_map/while/body/eval_jaxpr/psum | solution.py:16
  163.6 29.2 %reduce-scatter.2.cloned.1.call-start = ((), (), s32[]{:S(2)}) async-start(), calls=%async_computation.1 | async-start | bytes 1310720 | tf_op jit(solution)/shard_map/reduce_scatter | solution.py:59
  165.0 110.8 %all-reduce.6.cloned.1.call-start = ((), (), s32[]{:S(2)}) async-start(), calls=%async_computation.2 | async-start | bytes 131072 | tf_op jit(solution)/shard_map/psum | solution.py:9
  230.1 12.8 %copy-start.1 = (f32[512,128]{1,0:T(8,128)S(1)}, f32[512,128]{1,0:T(8,128)}, u32[]{:S(2)}) copy-start(f32[512,128]{1,0:T(8,128)} %reduce-scatter.2.cloned.1.call-done) | copy-start | bytes 786436
  230.1 13.7 %copy-start.3 = (s32[2,96]{1,0:T(2,128)S(1)}, s32[2,96]{1,0:T(2,128)}, u32[]{:S(2)}) copy-start(s32[2,96]{1,0:T(2,128)} %get-tuple-element.415) | copy-start | bytes 2308
  243.7 90.8 %all-reduce.10.cloned.1.call-start = ((), (), s32[]{:S(2)}) async-start(), calls=%async_computation.4 | async-start | bytes 2097152 | tf_op jit(solution)/shard_map/psum | solution.py:94
  252.4 136.7 %all-reduce.8.cloned.1.call-start = ((), (), s32[]{:S(2)}) async-start(), calls=%async_computation.3 | async-start | bytes 131072 | tf_op jit(solution)/shard_map/psum | solution.py:10
  275.8 154.4 %all-reduce.12.cloned.1.call-start = ((), (), s32[]{:S(2)}) async-start(), calls=%async_computation.5 | async-start | bytes 1048576 | tf_op jit(solution)/shard_map/psum | solution.py:16
Sparse Core Ops, SparseCore 0:
  20.8 57.2 all-reduce.13
  96.3 53.8 all-reduce.13
Sparse Core Ops, SparseCore 1:
  166.4 26.4 reduce-scatter.1
  243.8 31.9 all-reduce.5
  278.8 55.6 all-reduce.9
  337.6 51.4 all-reduce.7
  392.1 38.1 all-reduce.11
